TPU v7x, 128 devices: a whole 4x4x4 slice. The times are simulated.
128 devices in a mesh: req: 16 (over y, x), seq: 4 (over z), hid: 2 (over core).
Axes of the slice: x: 4, y: 4, z: 4, core: 2. Of those that a mesh axis runs over, the one named last changes fastest.
Arguments:
- tokens: bfloat16 [65536, 2048], P(('req', 'seq')), may hold values from -6 to 6
- attention_gain: bfloat16 [2048], replicated, may hold values from 0.099609375 to 1.8984375
- project_weight: bfloat16 [2048, 2048], P(None, 'hid'), may hold values from -0.125 to 0.125
- conv_weight: bfloat16 [4, 2048], P(None, 'hid'), may hold values from -3 to 3
- decay_down: bfloat16 [2048, 16], replicated, may hold values from -0.125 to 0.125
- decay_up: bfloat16 [16, 512], P(None, 'hid'), may hold values from -1.5 to 1.5
- decay_bias: float32 [512], P('hid'), may hold values from -2 to 10
- output_gate: bfloat16 [2048, 1024], P(None, 'hid'), may hold values from -0.125 to 0.125
- head_gain: bfloat16 [512], replicated, may hold values from 0.099609375 to 1.8984375
- output_weight: bfloat16 [1024, 2048], P('hid'), may hold values from -0.1875 to 0.1875
- mixer_gain: bfloat16 [2048], replicated, may hold values from 0.099609375 to 1.8984375
- gate_weight: bfloat16 [2048, 2816], P('req', 'hid'), may hold values from -0.125 to 0.125
- up_weight: bfloat16 [2048, 2816], P('req', 'hid'), may hold values from -0.125 to 0.125
- down_weight: bfloat16 [2816, 2048], P('hid', 'req'), may hold values from -0.109375 to 0.109375
- prompt_pages: int32 [16, 16], P('req'), may hold values from 0 to 64, as said below
- prompt_start: int32 [16, 16], P('req'), may hold values from 0 to 63, as said below
Outputs:
- hidden_out: bfloat16 [65536, 2048], P(('req', 'seq', 'hid'))
- page_states: bfloat16 [1024, 2, 256, 512], P(('req', 'seq'), 'hid')
- conv_edges: bfloat16 [1024, 3, 2048], P(('req', 'seq'), None, 'hid')
Inputs may be any that keep to these rules, and one draw needn't show every extreme that they name: `prompt_pages`: row r lists the page counts of the prompts of group r; 0 marks an unused slot; in every draw some group holds one prompt of all its 64 pages. `prompt_start`: the slots of a row that are used cover pages in increasing order without intersection and end by page 64; pages between prompts belong to none; an unused slot starts at page 64 - 1, and every draw has one.
All inputs are finite; a program needn't handle non-finite values.
Results may differ from a plain program's by a relative error of at most 0.014.
Values may be sent and summed in bfloat16 or wider, within the bound.
A program may use at most 192 MiB of HBM per device.

v0:
```python
import jax
import jax.numpy as jnp
from jax import lax
from jax.sharding import PartitionSpec as P

HK = 256
HV = 512
KCONV = 4
PAGE = 64
CONVW = 1024
EPSILON = 1e-06
TOP_PRECISION = lax.Precision.HIGHEST


def shifted(value, axis, steps):
    count = lax.axis_size(axis)
    first, last = (max(0, -steps), min(count, count - steps))
    return lax.ppermute(value, axis, [(source, source + steps) for source in range(first, last)])


def prefix_2(array, axis, join, neutral):
    place = lax.axis_index(axis)
    gathered = jax.tree.map(
        lambda a, kind: lax.all_gather(a.astype(kind), axis), array, (jnp.bfloat16, jnp.bfloat16)
    )
    state = jax.tree.map(lambda a, e: jnp.zeros_like(a) + jnp.asarray(e, a.dtype), array, neutral)

    def one(lap, state):
        return join(
            state,
            jax.tree.map(
                lambda a, own: lax.dynamic_index_in_dim(a, lap, 0, False).astype(own.dtype),
                gathered,
                array,
            ),
        )

    return lax.fori_loop(0, place, one, state)


def rms_scaled(values, scale_gain):
    values = values.astype(jnp.float32)
    return (
        values
        * lax.rsqrt(jnp.mean(values * values, axis=-1, keepdims=True) + EPSILON)
        * scale_gain.astype(jnp.float32)
    )


def page_segments(page_counts, starts, total_pages):
    position = jnp.arange(total_pages, dtype=jnp.int32)
    inside = (position[None, :] >= starts[:, None]) & (
        position[None, :] < starts[:, None] + page_counts[:, None]
    )
    labels = jnp.arange(1, page_counts.shape[0] + 1, dtype=jnp.int32)
    segment = jnp.sum(jnp.where(inside, labels[:, None], 0), axis=0) - 1
    earlier = jnp.concatenate([jnp.full((1,), -1, jnp.int32), segment[:-1]])
    return ((segment == earlier) & (segment >= 0)).astype(jnp.float32)


def short_conv(by_page, before, carried, conv_taps):
    kept_rows = before.astype(jnp.float32) * carried[:, None, None]
    widened = jnp.concatenate([kept_rows, by_page.astype(jnp.float32)], axis=1)
    tap_count = conv_taps.shape[0]
    length = by_page.shape[1]
    result = jnp.zeros(by_page.shape, jnp.float32)
    for offset in range(tap_count):
        result = (
            result
            + conv_taps[offset].astype(jnp.float32)
            * widened[:, tap_count - 1 - offset : tap_count - 1 - offset + length]
        )
    return result


def split_features(mixed_rows, key_width):
    query_rows = jax.nn.silu(mixed_rows[..., :key_width])
    key_rows = jax.nn.silu(mixed_rows[..., key_width : 2 * key_width]) * key_width ** (-0.5)
    value_matrix = mixed_rows[..., 2 * key_width :]
    return (
        query_rows.transpose(0, 2, 1, 3),
        key_rows.transpose(0, 2, 1, 3),
        value_matrix.transpose(0, 2, 1, 3),
    )


def page_block(query_rows, key_rows, value_matrix, decay_sum, carried):
    length = query_rows.shape[2]
    page_count = query_rows.shape[0]
    raised_rows = query_rows * jnp.exp(decay_sum)
    lowered = key_rows * jnp.exp(-decay_sum)
    scores = jnp.einsum("phik,phjk->phij", raised_rows, lowered, precision=TOP_PRECISION)
    rows_index = jnp.arange(length)
    causal = rows_index[:, None] >= rows_index[None, :]
    scores = jnp.where(causal[None, None], scores, 0.0)
    layer_output = jnp.einsum("phij,phjv->phiv", scores, value_matrix, precision=TOP_PRECISION)
    closing_sum = decay_sum[:, :, -1, :]
    weighted_rows = key_rows * jnp.exp(closing_sum[:, :, None, :] - decay_sum)
    page_terms = jnp.einsum("phte,phtb->pheb", weighted_rows, value_matrix, precision=TOP_PRECISION)
    through = jnp.cumsum(closing_sum, axis=0)
    resets = jnp.cumsum(1.0 - carried)
    pages = jnp.arange(page_count)
    valid = (pages[:, None] >= pages[None, :]) & (resets[:, None] == resets[None, :])
    spread = through[:, None] - through[None, :]
    spread = jnp.where(valid[:, :, None, None], spread, 0.0)
    weights = jnp.where(valid[:, :, None, None], jnp.exp(spread), 0.0)
    memories = jnp.einsum("pqhe,qheb->pheb", weights, page_terms, precision=TOP_PRECISION)
    previous = jnp.concatenate([jnp.zeros_like(memories[:1]), memories[:-1]], axis=0)
    previous = previous * carried[:, None, None, None]
    layer_output = layer_output + jnp.einsum(
        "phik,phkv->phiv", raised_rows, previous, precision=TOP_PRECISION
    )
    return (memories[-1], layer_output, memories)


def on_device(
    tokens,
    attention_gain,
    project_weight,
    conv_weight,
    decay_down,
    decay_up,
    decay_bias,
    output_gate,
    head_gain,
    output_weight,
    mixer_gain,
    gate_weight,
    up_weight,
    down_weight,
    prompt_pages,
    prompt_start,
):
    token_count = tokens.shape[0]
    page_count = token_count // PAGE
    local_heads = project_weight.shape[1] // CONVW
    rim_rows = KCONV - 1
    seq_index = lax.axis_index("seq")
    group_pages = page_count * lax.axis_size("seq")
    page_flags = page_segments(prompt_pages[0], prompt_start[0], group_pages)
    carried = lax.dynamic_slice_in_dim(page_flags, seq_index * page_count, page_count)
    normed = rms_scaled(tokens, attention_gain).astype(jnp.bfloat16)
    projected = jnp.dot(normed, project_weight, preferred_element_type=jnp.float32).astype(
        jnp.bfloat16
    )
    by_page = projected.reshape(page_count, PAGE, local_heads * CONVW)
    incoming = shifted(by_page[-1, PAGE - rim_rows :], "seq", 1)
    before = jnp.concatenate([incoming[None], by_page[:-1, PAGE - rim_rows :]], axis=0)
    mixed_rows = short_conv(by_page, before, carried, conv_weight).reshape(
        page_count, PAGE, local_heads, CONVW
    )
    query_rows, key_rows, value_matrix = split_features(mixed_rows, HK)
    gate_rows = lax.all_gather(gate_weight, "req", axis=0, tiled=True)
    up_rows = lax.all_gather(up_weight, "req", axis=0, tiled=True)
    down_columns = lax.all_gather(down_weight, "req", axis=1, tiled=True)
    gate_rows, query_rows = lax.optimization_barrier((gate_rows, query_rows))
    lowrank = jnp.dot(normed, decay_down, preferred_element_type=jnp.float32).astype(jnp.bfloat16)
    decay_log = (
        jax.nn.log_sigmoid(
            jnp.dot(lowrank, decay_up, preferred_element_type=jnp.float32) + decay_bias
        )
        / 16.0
    )
    decay_log = decay_log.reshape(page_count, PAGE, local_heads, HK).transpose(0, 2, 1, 3)
    decay_sum = jnp.cumsum(decay_log, axis=2)
    local_memory, outputs, memories = page_block(
        query_rows, key_rows, value_matrix, decay_sum, carried
    )
    totals = decay_sum[:, :, -1, :]
    through = jnp.cumsum(totals, axis=0)
    alive_mask = jnp.cumprod(carried)
    block_decay = alive_mask[-1] * jnp.exp(through[-1])

    def compose(earlier, latter):
        return (earlier[0] * latter[0], latter[0][..., None] * earlier[1] + latter[1])

    prefix = prefix_2(
        (block_decay, local_memory),
        "seq",
        compose,
        (jnp.ones_like(block_decay), jnp.zeros_like(local_memory)),
    )
    incoming_state = prefix[1]
    before_sum = through - totals
    extent_factor = alive_mask[:, None, None, None] * jnp.exp(decay_sum + before_sum[:, :, None, :])
    outputs = outputs + jnp.einsum(
        "dlof,lfg->dlog", query_rows * extent_factor, incoming_state, precision=TOP_PRECISION
    )
    memories = (
        memories + (alive_mask[:, None, None] * jnp.exp(through))[..., None] * incoming_state[None]
    )
    up_rows, outputs = lax.optimization_barrier((up_rows, outputs))
    attended = outputs.transpose(0, 2, 1, 3).reshape(token_count, local_heads, HV)
    normed_heads = rms_scaled(attended, head_gain)
    opening = jax.nn.silu(jnp.dot(normed, output_gate, preferred_element_type=jnp.float32)).reshape(
        token_count, local_heads, HV
    )
    gated_rows = (
        (normed_heads * opening).astype(jnp.bfloat16).reshape(token_count, local_heads * HV)
    )
    down_columns, gated_rows = lax.optimization_barrier((down_columns, gated_rows))
    partial_value = jnp.dot(gated_rows, output_weight, preferred_element_type=jnp.float32)
    half_rows = token_count // lax.axis_size("hid")
    row_start = lax.axis_index("hid") * half_rows
    mixed_sum = lax.psum(partial_value.astype(jnp.bfloat16), "hid").astype(jnp.float32)
    residual = (tokens.astype(jnp.float32) + mixed_sum).astype(jnp.bfloat16)
    feed_in = rms_scaled(residual, mixer_gain).astype(jnp.bfloat16)
    own_residual = lax.dynamic_slice_in_dim(residual, row_start, half_rows, 0)

    def widen(weight_rows):
        return jnp.dot(feed_in, weight_rows, preferred_element_type=jnp.float32)

    gate_part = widen(gate_rows)
    up_part = widen(up_rows)
    hidden = (jax.nn.silu(gate_part) * up_part).astype(jnp.bfloat16)
    partials = jnp.dot(hidden, down_columns, preferred_element_type=jnp.float32)
    feed_sum = lax.psum_scatter(
        partials.astype(jnp.bfloat16), "hid", scatter_dimension=0, tiled=True
    ).astype(jnp.float32)
    result = (own_residual.astype(jnp.float32) + feed_sum).astype(jnp.bfloat16)
    return (result, memories.astype(jnp.bfloat16), by_page[:, PAGE - rim_rows :])


def solution(mesh):
    return jax.shard_map(
        on_device,
        mesh=mesh,
        in_specs=(
            P(("req", "seq"), None),
            P(),
            P(None, "hid"),
            P(None, "hid"),
            P(),
            P(None, "hid"),
            P("hid"),
            P(None, "hid"),
            P(),
            P("hid", None),
            P(),
            P("req", "hid"),
            P("req", "hid"),
            P("hid", "req"),
            P("req", None),
            P("req", None),
        ),
        out_specs=(
            P(("req", "seq", "hid"), None),
            P(("req", "seq"), "hid", None, None),
            P(("req", "seq"), None, "hid"),
        ),
        check_vma=False,
    )
```

profile of v0, /device:TPU:1, one launch (start us, length us, event | category | flops | bytes accessed | tf_op | source)
XLA Modules:
  0.0 392.0 jit_solution(12662995687886767372)
XLA Ops:
  7.2 3.2 fusion.3
  10.5 0.3 copy-done.7
  10.8 7.3 %convolution_convert_fusion.2 = bf16[1024,1024]{1,0:T(8,128)(2,1)S(1)} fusion(bf16[2048,1024]{1,0:T(8,128)(2,1)} %param.20, bf16[1024,2048]{1,0:T(8,128)(2,1)S(1)} %copy-done.7, f32[2048]{0:T(1024)S(1)} %convert_element_type.149, f32[1024]{0:T(1024)S(1)} %add_rsqrt_fusion.2), kind=kOutput, calls=%fused_computation.53 | convolution fusion | flops 4304404480 | bytes 10498048 | tf_op jit(solution)/shard_map/dot_general | solution.py:143
  18.1 1.3 copy-done.10
  19.4 4.4 %collective-permute-start = (bf16[3,1024]{1,0:T(4,128)(2,1)S(1)}, bf16[3,1024]{1,0:T(4,128)(2,1)S(1)}, u32[]{:S(2)}, u32[]{:S(2)}) collective-permute-start(bf16[3,1024]{1,0:T(4,128)(2,1)S(1)} %slice_bitcast_fusion.5), channel_id=1, source_target_pairs={{0,2},{2,4},{4,6},{1,3},{3,5},{5,7},{8,10},{10,12},{12,14},{9,11},... | collective-permute-start | bytes 18440 | tf_op jit(solution)/shard_map/ppermute | solution.py:18
  23.9 0.1 select_reduce_fusion
  24.0 5.2 %fusion.37 = f32[1024,256]{1,0:T(8,128)} fusion(bf16[16,256]{1,0:T(8,128)(2,1)S(1)} %copy-done.18, bf16[2048,16]{0,1:T(8,128)(2,1)S(1)} %copy-done.17, f32[256]{0:T(256)S(1)} %copy-done.19, bf16[1024,2048]{1,0:T(8,128)(2,1)} %param.18, f32[2048]{0:T(1024)S(1)} %convert_element_type.149, f32[1024]{0:T(1024)S(1)} %add_rsqrt_fusion.2), kind=kOutput, calls=%fused_computation.60 | convolution fusion | flops 86523904 | bytes 5329920 | tf_op jit(solution)/shard_map/dot_general | solution.py:160
  29.2 1.8 fusion.49
  31.1 0.1 and_convert_fusion
  31.2 0.1 subtract_bitcast_fusion
  31.3 0.1 copy.65
  31.4 0.1 reduce.2
  31.5 0.1 fusion.72
  31.6 1.0 slice.80
  32.6 4.1 %convert_element_type.152 = f32[16,64,1024]{2,1,0:T(8,128)} convert(bf16[16,64,1024]{2,1,0:T(8,128)(2,1)} %bitcast.123) | non-fusion elementwise | flops 1048576 | bytes 6291456 | tf_op jit(solution)/shard_map/convert_element_type | solution.py:63
  36.7 0.1 copy.79
  36.8 0.1 convert_multiply_fusion.4
  36.9 7.6 %fusion.15 = f32[16,64,1,1024]{3,1,0,2:T(8,128)S(1)} fusion(f32[16,64,1024]{2,1,0:T(8,128)} %convert_element_type.152, f32[16,3,1024]{2,1,0:T(4,128)S(1)} %convert_multiply_fusion.4, f32[1024]{0:T(1024)S(1)} %bitcast.130, f32[1024]{0:T(1024)S(1)} %bitcast.131, f32[1024]{0:T(1024)S(1)} %bitcast.129, f32[1024]{0:T(1024)S(1)} %bitcast.128), kind=kLoop, calls=%fused_computation.29 | loop fusion | flops 10485760 | bytes 8601600 | tf_op jit(solution)/shard_map/reshape | solution.py:149
  44.6 7.4 %fusion.30 = f32[16,256,512]{2,1,0:T(8,128)S(1)} fusion(f32[16,64,1,1024]{3,1,0,2:T(8,128)S(1)} %fusion.15, f32[16,1,64,256]{3,0,1,2:T(8,128)S(1)} %fusion.49, f32[16,256]{1,0:T(8,128)S(1)} %get-tuple-element.97), kind=kOutput, calls=%fused_computation.51 | convolution fusion | flops 1612447744 | bytes 12599296 | tf_op jit(solution)/shard_map/phte,phtb->pheb/dot_general | solution.py:99
  52.0 13.6 %fusion.20 = f32[16,1,256,512]{3,0,2,1:T(8,128)S(1)} fusion(f32[16,256,512]{2,1,0:T(8,128)S(1)} %fusion.30, f32[16,256]{0,1:T(8,128)S(1)} %bitcast.125, pred[16,16]{1,0:T(8,128)(4,1)S(1)} %fusion.72), kind=kOutput, calls=%fused_computation.38 | convolution fusion | flops 402849792 | bytes 16793856 | tf_op jit(solution)/shard_map/pqhe,qheb->pheb/dot_general | solution.py:107
  65.6 3.2 copy-done.2
  68.8 0.6 slice.145
  69.4 0.7 copy.72
  70.1 0.0 all-gather.9.cloned.1.call-start
  70.2 0.7 all-gather.9.cloned.1.call-update
  70.9 0.0 all-gather.7.cloned.1.call-start
  70.9 0.7 all-gather.7.cloned.1.call-update
  71.7 0.5 all-gather.5.cloned.1.call-update
  72.2 0.0 all-reduce.3.cloned.1.call-start
  72.2 0.1 copy.71
  72.4 0.5 slice.90
  72.9 0.1 reduce.3
  73.0 0.6 fusion.74
  73.7 6.9 %all_gather.20 = bf16[4,1,256]{2,1,0:T(2,128)(2,1)S(1)} all-gather(bf16[1,1,256]{2,1,0:T(2,128)(2,1)S(1)} %fusion.74), channel_id=1, replica_groups=mesh['req'=16,'seq'=4,'hid'=2] {'seq'}, dimensions={0}, use_global_device_ids=true | all-gather | bytes 2560 | tf_op jit(solution)/shard_map/all_gather | solution.py:24
  80.6 2.5 multiply_bitcast_fusion.1
  83.1 8.6 %multiply_bitcast_fusion = f32[16,256,512]{2,0,1:T(8,128)} fusion(f32[15,1,256,512]{3,0,2,1:T(8,128)} %bitcast.119, f32[16]{0:T(128)S(1)} %get-tuple-element.95), kind=kLoop, calls=%fused_computation.19 | loop fusion | flops 2097152 | bytes 16252992 | tf_op jit(solution)/shard_map/reshape.33
  91.7 4.1 %all-gather.11.cloned.1.call-done = bf16[4,1,256,512]{3,2,1,0:T(8,128)(2,1)} async-done(((bf16[1,1,256,512]{3,2,1,0:T(8,128)(2,1)}), bf16[4,1,256,512]{3,2,1,0:T(8,128)(2,1)}) %all-gather.11.cloned.1.call-update) | async-done | bytes 1048592 | tf_op jit(solution)/shard_map/all_gather | solution.py:24
  95.8 0.2 while.12
  96.0 62.0 %all-gather.9.cloned.1.call-done = bf16[2048,1408]{1,0:T(8,128)(2,1)} async-done(((bf16[128,1408]{1,0:T(8,128)(2,1)}), bf16[2048,1408]{1,0:T(8,128)(2,1)}) %all-gather.9.cloned.1.call-update) | async-done | bytes 5767184 | tf_op jit(solution)/shard_map/all_gather | solution.py:153
  158.0 4.7 %convolution_select_fusion = f32[16,64,64]{2,1,0:T(8,128)S(1)} fusion(f32[16,1,64,256]{3,2,0,1:T(8,128)} %multiply_bitcast_fusion.1, f32[16,1,64,256]{3,0,1,2:T(8,128)} %copy-done.5, pred[64,64]{1,0:T(8,128)(4,1)S(1)} %iota_compare_fusion, f32[16,64,1,1024]{3,1,0,2:T(8,128)} %copy-done.4), kind=kOutput, calls=%fused_computation.56 | convolution fusion | flops 203489280 | bytes 4460544 | tf_op jit(solution)/shard_map/phik,phjk->phij/dot_general | solution.py:92
  162.7 3.4 fusion.31
  166.2 10.6 %fusion.7 = f32[16,64,512]{2,1,0:T(8,128)S(1)} fusion(f32[16,256,512]{2,0,1:T(8,128)S(1)} %copy-done.3, f32[16,1,64,256]{3,2,0,1:T(8,128)S(1)} %copy-done.8, f32[16,1,64,256]{3,0,1,2:T(8,128)S(1)} %copy-done.6), kind=kOutput, calls=%fused_computation.14 | convolution fusion | flops 1610874880 | bytes 12582912 | tf_op jit(solution)/shard_map/phik,phkv->phiv/dot_general | solution.py:110
  176.7 3.9 bitcast_add_fusion
  180.6 38.0 %all-gather.7.cloned.1.call-done = bf16[2048,1408]{1,0:T(8,128)(2,1)} async-done(((bf16[128,1408]{1,0:T(8,128)(2,1)}), bf16[2048,1408]{1,0:T(8,128)(2,1)}) %all-gather.7.cloned.1.call-update) | async-done | bytes 5767184 | tf_op jit(solution)/shard_map/all_gather | solution.py:154
  218.6 1.8 multiply_reduce_fusion
  220.4 0.1 rsqrt.29
  220.5 7.1 %fusion.25 = bf16[1024,512]{1,0:T(8,128)(2,1)} fusion(f32[16,1,64,512]{3,2,0,1:T(8,128)} %bitcast_add_fusion, f32[512]{0:T(512)S(1)} %convert_element_type.163, f32[1024]{0:T(1024)S(1)} %rsqrt.29, bf16[2048,512]{1,0:T(8,128)(2,1)} %param.25, bf16[1024,2048]{1,0:T(8,128)(2,1)} %param.18, f32[2048]{0:T(1024)S(1)} %convert_element_type.149, ...), kind=kOutput, calls=%fused_computation.45 | convolution fusion | flops 2160066560 | bytes 9455616 | tf_op jit(solution)/shard_map/dot_general | solution.py:195
  227.6 56.9 %all-gather.5.cloned.1.call-done = bf16[1408,2048]{1,0:T(8,128)(2,1)} async-done(((bf16[1408,128]{1,0:T(8,128)(2,1)}), bf16[1408,2048]{1,0:T(8,128)(2,1)}) %all-gather.5.cloned.1.call-update) | async-done | bytes 5767184 | tf_op jit(solution)/shard_map/all_gather | solution.py:155
  284.5 5.6 %convolution_convert_fusion.1 = bf16[1024,2048]{1,0:T(8,128)(2,1)} fusion(bf16[1024,512]{1,0:T(8,128)(2,1)} %fusion.25, bf16[512,2048]{1,0:T(8,128)(2,1)S(1)} %copy-done), kind=kOutput, calls=%fused_computation.37 | convolution fusion | flops 2149580800 | bytes 7340032 | tf_op jit(solution)/shard_map/dot_general | solution.py:202
  290.2 0.0 reduce-scatter.2.cloned.1.call-start
  290.2 0.6 copy-done.13
  290.8 34.2 %all-reduce.3.cloned.1.call-done = bf16[1024,2048]{1,0:T(8,128)(2,1)} async-done(((bf16[1024,2048]{1,0:T(8,128)(2,1)}), bf16[1024,2048]{1,0:T(8,128)(2,1)}) %all-reduce.3.cloned.1.call-update) | async-done | bytes 4194320 | tf_op jit(solution)/shard_map/psum | solution.py:205
  325.0 5.5 %fusion = (f32[1024]{0:T(1024)S(1)}, bf16[1024,2048]{1,0:T(8,128)(2,1)S(1)}) fusion(bf16[1024,2048]{1,0:T(8,128)(2,1)} %all-reduce.3.cloned.1.call-done, bf16[1024,2048]{1,0:T(8,128)(2,1)} %param.18), kind=kLoop, calls=%fused_computation.7 | loop fusion | flops 14679040 | bytes 12587008 | tf_op jit(solution)/shard_map/reduce_sum | solution.py:45
  330.5 2.0 copy-done.9
  332.5 10.7 %fusion.34 = f32[1024,1408]{1,0:T(8,128)} fusion(bf16[2048,1408]{1,0:T(8,128)(2,1)} %all-gather.9.cloned.1.call-done, bf16[1024,2048]{1,0:T(8,128)(2,1)S(1)} %get-tuple-element.93, f32[2048]{0:T(1024)S(1)} %convert_element_type.170, f32[1024]{0:T(1024)S(1)} %add_rsqrt_fusion.1), kind=kOutput, calls=%fused_computation.57 | convolution fusion | flops 5913968640 | bytes 15740928 | tf_op jit(solution)/shard_map/dot_general | solution.py:211
  343.2 20.9 %convolution_convert_fusion = bf16[1024,2048]{1,0:T(8,128)(2,1)} fusion(bf16[1408,2048]{1,0:T(8,128)(2,1)} %all-gather.5.cloned.1.call-done, f32[1024,1408]{1,0:T(8,128)} %fusion.34, bf16[2048,1408]{1,0:T(8,128)(2,1)} %all-gather.7.cloned.1.call-done, bf16[1024,2048]{1,0:T(8,128)(2,1)} %copy-done.9, f32[2048]{0:T(1024)S(1)} %convert_element_type.170, ...), kind=kOutput, calls=%fused_computation.36 | convolution fusion | flops 11830296576 | bytes 25702400 | tf_op jit(solution)/shard_map/dot_general | solution.py:216
  364.1 1.0 slice.93
  365.2 0.1 fusion.68
  365.2 0.1 copy.74
  365.3 0.7 copy.76
  366.0 4.0 %add_convert_fusion = bf16[16,1,256,512]{3,0,2,1:T(8,128)(2,1)S(1)} fusion(f32[16,1,256,512]{3,0,2,1:T(8,128)} %copy-done.2, f32[256,512]{1,0:T(8,128)S(1)} %bitcast.120, f32[16,256]{0,1:T(8,128)S(1)} %copy.74), kind=kLoop, calls=%fused_computation.18 | loop fusion | flops 6291456 | bytes 13123584 | tf_op jit(solution)/shard_map/convert_element_type | solution.py:221
  370.0 4.5 %copy.75 = bf16[16,1,256,512]{3,2,1,0:T(8,128)(2,1)} copy(bf16[16,1,256,512]{3,0,2,1:T(8,128)(2,1)S(1)} %add_convert_fusion) | data formatting | bytes 8388608
  374.5 5.8 %reduce-scatter.2.cloned.1.call-done = bf16[512,2048]{1,0:T(8,128)(2,1)} async-done(((bf16[1024,2048]{1,0:T(8,128)(2,1)}), bf16[512,2048]{1,0:T(8,128)(2,1)}) %reduce-scatter.2.cloned.1.call-update) | async-done | bytes 2097168 | tf_op jit(solution)/shard_map/reduce_scatter | solution.py:217
  380.3 4.4 %add_convert_fusion.1 = bf16[512,2048]{1,0:T(8,128)(2,1)} fusion(bf16[512,2048]{1,0:T(8,128)(2,1)} %reduce-scatter.2.cloned.1.call-done, bf16[1024,2048]{1,0:T(8,128)(2,1)} %copy-done.9, s32[]{:T(128)S(6)} %select_n.46), kind=kLoop, calls=%fused_computation.35 | loop fusion | flops 4194304 | bytes 6291460 | tf_op jit(solution)/shard_map/convert_element_type | solution.py:220
  (58 shorter events, 0.4 us)
Async XLA Ops:
  7.2 277.4 %copy-start = (bf16[512,2048]{1,0:T(8,128)(2,1)S(1)}, bf16[512,2048]{1,0:T(8,128)(2,1)}, u32[]{:S(2)}) copy-start(bf16[512,2048]{1,0:T(8,128)(2,1)} %param.27) | copy-start | bytes 6291460
  7.2 3.3 copy-start.12
  7.2 88.6 %all-gather.11.cloned.1.call-start = ((), (), s32[]{:S(2)}) async-start(), calls=%async_computation.4 | async-start | bytes 1310720 | tf_op jit(solution)/shard_map/all_gather | solution.py:24
  7.2 3.6 copy-start.7
  10.8 13.0 %copy-start.14 = (s32[1,16]{1,0:T(1,128)S(1)}, s32[1,16]{1,0:T(1,128)}, u32[]{:S(2)}) copy-start(s32[1,16]{1,0:T(1,128)} %param.33) | copy-start | bytes 196
  10.8 13.0 %copy-start.16 = (s32[1,16]{1,0:T(1,128)S(1)}, s32[1,16]{1,0:T(1,128)}, u32[]{:S(2)}) copy-start(s32[1,16]{1,0:T(1,128)} %param.32) | copy-start | bytes 196
  10.8 13.2 %copy-start.11 = (bf16[4,1024]{1,0:T(4,128)(2,1)S(1)}, bf16[4,1024]{1,0:T(4,128)(2,1)}, u32[]{:S(2)}) copy-start(bf16[4,1024]{1,0:T(4,128)(2,1)} %param.21) | copy-start | bytes 24580
  10.8 13.2 %copy-start.17 = (bf16[2048,16]{0,1:T(8,128)(2,1)S(1)}, bf16[2048,16]{0,1:T(8,128)(2,1)}, u32[]{:S(2)}) copy-start(bf16[2048,16]{0,1:T(8,128)(2,1)} %param.22) | copy-start | bytes 196612
  10.8 13.2 %copy-start.18 = (bf16[16,256]{1,0:T(8,128)(2,1)S(1)}, bf16[16,256]{1,0:T(8,128)(2,1)}, u32[]{:S(2)}) copy-start(bf16[16,256]{1,0:T(8,128)(2,1)} %param.23) | copy-start | bytes 24580
  10.8 13.2 %copy-start.19 = (f32[256]{0:T(256)S(1)}, f32[256]{0:T(256)}, u32[]{:S(2)}) copy-start(f32[256]{0:T(256)} %param.24) | copy-start | bytes 3076
  18.1 1.3 copy-start.10
  19.4 17.3 %collective-permute-start = (bf16[3,1024]{1,0:T(4,128)(2,1)S(1)}, bf16[3,1024]{1,0:T(4,128)(2,1)S(1)}, u32[]{:S(2)}, u32[]{:S(2)}) collective-permute-start(bf16[3,1024]{1,0:T(4,128)(2,1)S(1)} %slice_bitcast_fusion.5), channel_id=1, source_target_pairs={{0,2},{2,4},{4,6},{1,3},{3,5},{5,7},{8,10},{10,12},{12,14},{9,11},... | collective-permute-start | bytes 18440 | tf_op jit(solution)/shard_map/ppermute | solution.py:18
  31.0 13.5 %copy-start.5 = (f32[16,1,64,256]{3,0,1,2:T(8,128)}, f32[16,1,64,256]{3,0,1,2:T(8,128)S(1)}, u32[]{:S(2)}) copy-start(f32[16,1,64,256]{3,0,1,2:T(8,128)S(1)} %fusion.49) | copy-start | bytes 3145732
  44.6 7.4 %copy-start.4 = (f32[16,64,1,1024]{3,1,0,2:T(8,128)}, f32[16,64,1,1024]{3,1,0,2:T(8,128)S(1)}, u32[]{:S(2)}) copy-start(f32[16,64,1,1024]{3,1,0,2:T(8,128)S(1)} %fusion.15) | copy-start | bytes 12582916
  52.0 21.1 %copy-start.15 = (bf16[512]{0:T(512)(128)(2,1)S(1)}, bf16[512]{0:T(512)(128)(2,1)}, u32[]{:S(2)}) copy-start(bf16[512]{0:T(512)(128)(2,1)} %param.26) | copy-start | bytes 3076
  65.6 3.2 copy-start.2
  70.1 87.9 %all-gather.9.cloned.1.call-start = ((), (), s32[]{:S(2)}) async-start(), calls=%async_computation.3 | async-start | bytes 6127616 | tf_op jit(solution)/shard_map/all_gather | solution.py:153
  70.9 147.7 %all-gather.7.cloned.1.call-start = ((), (), s32[]{:S(2)}) async-start(), calls=%async_computation.2 | async-start | bytes 6127616 | tf_op jit(solution)/shard_map/all_gather | solution.py:154
  71.6 212.9 %all-gather.5.cloned.1.call-start = ((), (), s32[]{:S(2)}) async-start(), calls=%async_computation.1 | async-start | bytes 6127616 | tf_op jit(solution)/shard_map/all_gather | solution.py:155
  72.2 252.8 %all-reduce.3.cloned.1.call-start = ((), (), s32[]{:S(2)}) async-start(), calls=%async_computation.5 | async-start | bytes 8388608 | tf_op jit(solution)/shard_map/psum | solution.py:205
  158.0 8.2 %copy-start.3 = (f32[16,256,512]{2,0,1:T(8,128)S(1)}, f32[16,256,512]{2,0,1:T(8,128)}, u32[]{:S(2)}) copy-start(f32[16,256,512]{2,0,1:T(8,128)} %multiply_bitcast_fusion) | copy-start | bytes 25165828
  158.0 8.2 %copy-start.6 = (f32[16,1,64,256]{3,0,1,2:T(8,128)S(1)}, f32[16,1,64,256]{3,0,1,2:T(8,128)}, u32[]{:S(2)}) copy-start(f32[16,1,64,256]{3,0,1,2:T(8,128)} %copy-done.5) | copy-start | bytes 3145732
  158.0 8.2 %copy-start.8 = (f32[16,1,64,256]{3,2,0,1:T(8,128)S(1)}, f32[16,1,64,256]{3,2,0,1:T(8,128)}, u32[]{:S(2)}) copy-start(f32[16,1,64,256]{3,2,0,1:T(8,128)} %multiply_bitcast_fusion.1) | copy-start | bytes 3145732
  290.1 0.7 copy-start.13
  290.2 90.2 %reduce-scatter.2.cloned.1.call-start = ((), (), s32[]{:S(2)}) async-start(), calls=%async_computation.6 | async-start | bytes 6291456 | tf_op jit(solution)/shard_map/reduce_scatter | solution.py:217
  330.5 2.0 copy-start.9
  370.0 14.8 %copy-start.1 = (bf16[512,2048]{1,0:T(8,128)(2,1)S(1)}, bf16[512,2048]{1,0:T(8,128)(2,1)}, u32[]{:S(2)}) copy-start(bf16[512,2048]{1,0:T(8,128)(2,1)} %param.27) | copy-start | bytes 6291460
Sparse Core Ops, SparseCore 0:
  70.2 25.4 all-gather.10
  97.9 60.0 all-gather.8
  160.1 58.4 all-gather.6
  220.6 63.9 all-gather.4
  290.3 34.7 all-reduce.2
  364.2 16.0 reduce-scatter.1
where the time goes:
time: 398 us; the launch traced here: 392 us
  waiting for transfers between devices  203 us (51%)
  matrix products  100 us (25%)
  other arithmetic  45.1 us (11%)
  local copies, waits for them, and re-layouts  17 us (4%)
  between operations  15 us (4%)
  blocking collectives  6.9 us (2%)
  starting transfers between devices  4.61 us (1%)
    all_gather x1, waiting for transfers between devices, on_device(): gate_rows = lax.all_gather(gate_weight, 'req', axis=0, tiled=True)  62 us
    all_gather x1, waiting for transfers between devices, on_device(): down_columns = lax.all_gather(down_weight, 'req', axis=1, tiled=True)  56.9 us
    all_gather x1, waiting for transfers between devices, on_device(): up_rows = lax.all_gather(up_weight, 'req', axis=0, tiled=True)  38 us
    psum x1, waiting for transfers between devices, on_device(): lax.psum(partial_value.astype(jnp.bfloat16), 'hid').astype(jnp.float32)  34.2 us
    dot_general x1, matrix products, on_device(): partials = jnp.dot(hidden, down_columns, preferred_element_type=jnp.float32)  20.9 us
    dot_general x1, matrix products, page_block(): jnp.einsum('pqhe,qheb->pheb', weights, page_terms, precision=TOP_PRECISION)  13.6 us
    unnamed x43, local copies, waits for them, and re-layouts  12.8 us
    dot_general x1, matrix products, widen(): return jnp.dot(feed_in, weight_rows, preferred_element_type=jnp.float32)  10.7 us
  transfers between devices with their start and end apart: 7, of which 6 were waited for; matrix products, arithmetic and copies ran while one was open for 17% of the time, Pallas kernels for 0%

commit v1 on v0

--- a/solution.py
+++ b/solution.py
@@ -150,8 +150,12 @@
         page_count, PAGE, local_heads, CONVW
     )
     query_rows, key_rows, value_matrix = split_features(mixed_rows, HK)
-    gate_rows = lax.all_gather(gate_weight, "req", axis=0, tiled=True)
-    up_rows = lax.all_gather(up_weight, "req", axis=0, tiled=True)
+    list_modes = lambda s0, group_axis, w_in: jnp.split(
+        lax.all_gather(jnp.concatenate([s0, w_in], 1), group_axis, axis=0, tiled=True),
+        [s0.shape[1]],
+        1,
+    )
+    gate_rows, up_rows = list_modes(gate_weight, "req", up_weight)
     down_columns = lax.all_gather(down_weight, "req", axis=1, tiled=True)
     gate_rows, query_rows = lax.optimization_barrier((gate_rows, query_rows))
     lowrank = jnp.dot(normed, decay_down, preferred_element_type=jnp.float32).astype(jnp.bfloat16)

time: 398 us -> 365 us (0.917)
  waiting for transfers between devices: 203 us -> 158 us
  local copies, waits for them, and re-layouts: 17 us -> 27.4 us
    all_gather x1, waiting for transfers between devices: 56.9 us -> 24.7 us  [on_device(): down_columns = lax.all_gather(down_weight, 'req', axis=1, tiled=True)]
    all_gather x2 -> x1, waiting for transfers between devices: 99.9 us -> 88.3 us  [on_device(): lax.all_gather(jnp.concatenate([s0, w_in], 1), group_axis, axis=0, tiled=...]
    split x0 -> x1, local copies, waits for them, and re-layouts: none -> 9.36 us  [on_device(): jnp.split(lax.all_gather(jnp.concatenate([s0, w_in], 1), group_axis, axis...]
    unnamed x43 -> x47, local copies, waits for them, and re-layouts: 12.8 us -> 13.8 us
  transfers between devices with their start and end apart: 7 -> 6, of which waited for: 6 -> 5; matrix products, arithmetic and copies ran while one was open for 17% -> 21% of each run, Pallas kernels for 0% -> 0%
where the time goes in v1:
time: 365 us; the launch traced here: 358 us
  waiting for transfers between devices  158 us (43%)
  matrix products  101 us (28%)
  other arithmetic  45.5 us (12%)
  local copies, waits for them, and re-layouts  27.4 us (8%)
  between operations  14.7 us (4%)
  blocking collectives  6.9 us (2%)
  starting transfers between devices  4.57 us (1%)
    all_gather x1, waiting for transfers between devices, on_device(): lax.all_gather(jnp.concatenate([s0, w_in], 1), group_axis, axis=0, tiled=...  88.3 us
    psum x1, waiting for transfers between devices, on_device(): lax.psum(partial_value.astype(jnp.bfloat16), 'hid').astype(jnp.float32)  34.2 us
    all_gather x1, waiting for transfers between devices, on_device(): down_columns = lax.all_gather(down_weight, 'req', axis=1, tiled=True)  24.7 us
    dot_general x1, matrix products, on_device(): partials = jnp.dot(hidden, down_columns, preferred_element_type=jnp.float32)  20.9 us
    unnamed x47, local copies, waits for them, and re-layouts  13.8 us
    dot_general x1, matrix products, page_block(): jnp.einsum('phik,phkv->phiv', raised_rows, previous, precision=TOP_PRECIS...  13.7 us
    dot_general x1, matrix products, page_block(): jnp.einsum('pqhe,qheb->pheb', weights, page_terms, precision=TOP_PRECISION)  13.6 us
    dot_general x1, matrix products, widen(): return jnp.dot(feed_in, weight_rows, preferred_element_type=jnp.float32)  10.7 us
  transfers between devices with their start and end apart: 6, of which 5 were waited for; matrix products, arithmetic and copies ran while one was open for 21% of the time, Pallas kernels for 0%

profile of v1, /device:TPU:1, one launch (start us, length us, event | category | flops | bytes accessed | tf_op | source)
XLA Modules:
  0.0 358.4 jit_solution(5242208729086664033)
XLA Ops:
  7.2 0.8 convert_element_type.149
  8.1 3.4 fusion.3
  11.6 7.2 %convolution_convert_fusion.2 = bf16[1024,1024]{1,0:T(8,128)(2,1)S(1)} fusion(bf16[2048,1024]{1,0:T(8,128)(2,1)} %param.20, bf16[1024,2048]{1,0:T(8,128)(2,1)S(1)} %copy-done.7, f32[2048]{0:T(1024)S(1)} %convert_element_type.149, f32[1024]{0:T(1024)S(1)} %add_rsqrt_fusion.2), kind=kOutput, calls=%fused_computation.53 | convolution fusion | flops 4304404480 | bytes 10498048 | tf_op jit(solution)/shard_map/dot_general | solution.py:143
  18.8 1.3 copy-done.11
  20.2 4.4 %collective-permute-start = (bf16[3,1024]{1,0:T(4,128)(2,1)S(1)}, bf16[3,1024]{1,0:T(4,128)(2,1)S(1)}, u32[]{:S(2)}, u32[]{:S(2)}) collective-permute-start(bf16[3,1024]{1,0:T(4,128)(2,1)S(1)} %slice_bitcast_fusion.5), channel_id=1, source_target_pairs={{0,2},{2,4},{4,6},{1,3},{3,5},{5,7},{8,10},{10,12},{12,14},{9,11},... | collective-permute-start | bytes 18440 | tf_op jit(solution)/shard_map/ppermute | solution.py:18
  24.6 0.1 select_reduce_fusion
  24.7 5.2 %fusion.37 = f32[1024,256]{1,0:T(8,128)} fusion(bf16[16,256]{1,0:T(8,128)(2,1)S(1)} %copy-done.20, bf16[2048,16]{0,1:T(8,128)(2,1)S(1)} %copy-done.19, f32[256]{0:T(256)S(1)} %copy-done.21, bf16[1024,2048]{1,0:T(8,128)(2,1)} %param.18, f32[2048]{0:T(1024)S(1)} %convert_element_type.149, f32[1024]{0:T(1024)S(1)} %add_rsqrt_fusion.2), kind=kOutput, calls=%fused_computation.60 | convolution fusion | flops 86523904 | bytes 5329920 | tf_op jit(solution)/shard_map/dot_general | solution.py:164
  29.9 1.8 fusion.49
  31.8 0.1 and_convert_fusion
  31.9 0.1 subtract_bitcast_fusion
  32.0 0.1 copy.65
  32.1 0.1 reduce.2
  32.2 0.1 fusion.72
  32.3 4.1 %convert_element_type.152 = f32[16,64,1024]{2,1,0:T(8,128)} convert(bf16[16,64,1024]{2,1,0:T(8,128)(2,1)} %bitcast.122) | non-fusion elementwise | flops 1048576 | bytes 6291456 | tf_op jit(solution)/shard_map/convert_element_type | solution.py:63
  36.4 1.0 slice.80
  37.4 0.1 copy.79
  37.5 0.1 convert_multiply_fusion.4
  37.6 7.7 %fusion.15 = f32[16,64,1,1024]{3,1,0,2:T(8,128)S(1)} fusion(f32[16,64,1024]{2,1,0:T(8,128)} %convert_element_type.152, f32[16,3,1024]{2,1,0:T(4,128)S(1)} %convert_multiply_fusion.4, f32[1024]{0:T(1024)S(1)} %bitcast.130, f32[1024]{0:T(1024)S(1)} %bitcast.131, f32[1024]{0:T(1024)S(1)} %bitcast.129, f32[1024]{0:T(1024)S(1)} %bitcast.128), kind=kLoop, calls=%fused_computation.29 | loop fusion | flops 10485760 | bytes 8601600 | tf_op jit(solution)/shard_map/reshape | solution.py:149
  45.3 7.4 %fusion.30 = f32[16,256,512]{2,1,0:T(8,128)S(1)} fusion(f32[16,64,1,1024]{3,1,0,2:T(8,128)S(1)} %fusion.15, f32[16,1,64,256]{3,0,1,2:T(8,128)S(1)} %fusion.49, f32[16,256]{1,0:T(8,128)S(1)} %get-tuple-element.99), kind=kOutput, calls=%fused_computation.51 | convolution fusion | flops 1612447744 | bytes 12599296 | tf_op jit(solution)/shard_map/phte,phtb->pheb/dot_general | solution.py:99
  52.7 13.6 %fusion.20 = f32[16,1,256,512]{3,0,2,1:T(8,128)S(1)} fusion(f32[16,256,512]{2,1,0:T(8,128)S(1)} %fusion.30, f32[16,256]{0,1:T(8,128)S(1)} %bitcast.125, pred[16,16]{1,0:T(8,128)(4,1)S(1)} %fusion.72), kind=kOutput, calls=%fused_computation.38 | convolution fusion | flops 402849792 | bytes 16793856 | tf_op jit(solution)/shard_map/pqhe,qheb->pheb/dot_general | solution.py:107
  66.3 3.3 copy-done.2
  69.6 0.6 slice.145
  70.1 0.7 copy.72
  70.9 0.0 all-gather.6.cloned.1.call-start
  71.0 0.9 pad_maximum_fusion.1
  71.9 0.0 all-gather.4.cloned.1.call-start
  72.0 0.7 all-gather.4.cloned.1.call-update
  72.7 0.0 all-reduce.3.cloned.1.call-start
  72.7 0.1 copy.71
  72.8 0.5 slice.90
  73.3 0.1 reduce.3
  73.5 0.6 fusion.74
  74.0 6.9 %all_gather.16 = bf16[4,1,256]{2,1,0:T(2,128)(2,1)S(1)} all-gather(bf16[1,1,256]{2,1,0:T(2,128)(2,1)S(1)} %fusion.74), channel_id=1, replica_groups=mesh['req'=16,'seq'=4,'hid'=2] {'seq'}, dimensions={0}, use_global_device_ids=true | all-gather | bytes 2560 | tf_op jit(solution)/shard_map/all_gather | solution.py:24
  81.0 2.5 multiply_bitcast_fusion.1
  83.5 8.7 %multiply_bitcast_fusion = f32[16,256,512]{2,0,1:T(8,128)} fusion(f32[15,1,256,512]{3,0,2,1:T(8,128)} %bitcast.119, f32[16]{0:T(128)S(1)} %get-tuple-element.95), kind=kLoop, calls=%fused_computation.19 | loop fusion | flops 2097152 | bytes 16252992 | tf_op jit(solution)/shard_map/reshape.33
  92.2 4.4 %all-gather.8.cloned.1.call-done = bf16[4,1,256,512]{3,2,1,0:T(8,128)(2,1)} async-done(((bf16[1,1,256,512]{3,2,1,0:T(8,128)(2,1)}), bf16[4,1,256,512]{3,2,1,0:T(8,128)(2,1)}) %all-gather.8.cloned.1.call-update) | async-done | bytes 1048592 | tf_op jit(solution)/shard_map/all_gather | solution.py:24
  96.6 0.2 while.12
  96.8 88.3 %all-gather.6.cloned.1.call-done = bf16[2048,2816]{1,0:T(8,128)(2,1)} async-done(((bf16[128,2816]{1,0:T(8,128)(2,1)}), bf16[2048,2816]{1,0:T(8,128)(2,1)}) %all-gather.6.cloned.1.call-update) | async-done | bytes 11534352 | tf_op jit(solution)/shard_map/all_gather | solution.py:154
  185.1 9.4 %fusion.88 = (bf16[2048,1408]{1,0:T(8,128)(2,1)}, bf16[2048,1408]{1,0:T(8,128)(2,1)}) fusion(bf16[2048,2816]{1,0:T(8,128)(2,1)} %all-gather.6.cloned.1.call-done), kind=kLoop, calls=%fused_computation.133 | loop fusion | bytes 23068672 | tf_op jit(solution)/shard_map/split | solution.py:153
  194.5 4.8 %convolution_select_fusion = f32[16,64,64]{2,1,0:T(8,128)S(1)} fusion(f32[16,1,64,256]{3,2,0,1:T(8,128)} %multiply_bitcast_fusion.1, f32[16,1,64,256]{3,0,1,2:T(8,128)} %copy-done.5, pred[64,64]{1,0:T(8,128)(4,1)S(1)} %iota_compare_fusion, f32[16,64,1,1024]{3,1,0,2:T(8,128)} %copy-done.3), kind=kOutput, calls=%fused_computation.56 | convolution fusion | flops 203489280 | bytes 4460544 | tf_op jit(solution)/shard_map/phik,phjk->phij/dot_general | solution.py:92
  199.3 1.8 fusion.31
  201.2 13.7 %fusion.7 = f32[16,64,512]{2,1,0:T(8,128)S(1)} fusion(f32[16,256,512]{2,0,1:T(8,128)} %multiply_bitcast_fusion, f32[16,1,64,256]{3,2,0,1:T(8,128)S(1)} %copy-done.8, f32[16,1,64,256]{3,0,1,2:T(8,128)S(1)} %copy-done.6), kind=kOutput, calls=%fused_computation.14 | convolution fusion | flops 1610874880 | bytes 12582912 | tf_op jit(solution)/shard_map/phik,phkv->phiv/dot_general | solution.py:110
  214.9 2.6 bitcast_add_fusion
  217.5 1.3 copy-done.10
  218.8 0.2 multiply_reduce_fusion
  219.0 0.1 rsqrt.29
  219.1 7.4 %fusion.25 = bf16[1024,512]{1,0:T(8,128)(2,1)} fusion(f32[16,1,64,512]{3,2,0,1:T(8,128)} %copy-done.10, f32[512]{0:T(512)S(1)} %convert_element_type.163, f32[1024]{0:T(1024)S(1)} %rsqrt.29, bf16[2048,512]{1,0:T(8,128)(2,1)} %param.25, bf16[1024,2048]{1,0:T(8,128)(2,1)} %param.18, f32[2048]{0:T(1024)S(1)} %convert_element_type.149, ...), kind=kOutput, calls=%fused_computation.45 | convolution fusion | flops 2160066560 | bytes 9455616 | tf_op jit(solution)/shard_map/dot_general | solution.py:199
  226.6 24.7 %all-gather.4.cloned.1.call-done = bf16[1408,2048]{1,0:T(8,128)(2,1)} async-done(((bf16[1408,128]{1,0:T(8,128)(2,1)}), bf16[1408,2048]{1,0:T(8,128)(2,1)}) %all-gather.4.cloned.1.call-update) | async-done | bytes 5767184 | tf_op jit(solution)/shard_map/all_gather | solution.py:159
  251.2 5.6 %convolution_convert_fusion.1 = bf16[1024,2048]{1,0:T(8,128)(2,1)} fusion(bf16[1024,512]{1,0:T(8,128)(2,1)} %fusion.25, bf16[512,2048]{1,0:T(8,128)(2,1)S(1)} %copy-done), kind=kOutput, calls=%fused_computation.37 | convolution fusion | flops 2149580800 | bytes 7340032 | tf_op jit(solution)/shard_map/dot_general | solution.py:206
  256.8 0.0 reduce-scatter.2.cloned.1.call-start
  256.9 0.6 copy-done.15
  257.5 34.2 %all-reduce.3.cloned.1.call-done = bf16[1024,2048]{1,0:T(8,128)(2,1)} async-done(((bf16[1024,2048]{1,0:T(8,128)(2,1)}), bf16[1024,2048]{1,0:T(8,128)(2,1)}) %all-reduce.3.cloned.1.call-update) | async-done | bytes 4194320 | tf_op jit(solution)/shard_map/psum | solution.py:209
  291.8 5.5 %fusion = (f32[1024]{0:T(1024)S(1)}, bf16[1024,2048]{1,0:T(8,128)(2,1)S(1)}) fusion(bf16[1024,2048]{1,0:T(8,128)(2,1)} %all-reduce.3.cloned.1.call-done, bf16[1024,2048]{1,0:T(8,128)(2,1)} %param.18), kind=kLoop, calls=%fused_computation.7 | loop fusion | flops 14679040 | bytes 12587008 | tf_op jit(solution)/shard_map/reduce_sum | solution.py:45
  297.2 1.9 copy-done.9
  299.2 10.7 %fusion.34 = f32[1024,1408]{1,0:T(8,128)} fusion(bf16[2048,1408]{1,0:T(8,128)(2,1)} %get-tuple-element.57, bf16[1024,2048]{1,0:T(8,128)(2,1)S(1)} %get-tuple-element.93, f32[2048]{0:T(1024)S(1)} %convert_element_type.170, f32[1024]{0:T(1024)S(1)} %add_rsqrt_fusion.1), kind=kOutput, calls=%fused_computation.57 | convolution fusion | flops 5913968640 | bytes 15740928 | tf_op jit(solution)/shard_map/dot_general | solution.py:215
  309.9 20.9 %convolution_convert_fusion = bf16[1024,2048]{1,0:T(8,128)(2,1)} fusion(bf16[1408,2048]{1,0:T(8,128)(2,1)} %all-gather.4.cloned.1.call-done, f32[1024,1408]{1,0:T(8,128)} %fusion.34, bf16[2048,1408]{1,0:T(8,128)(2,1)} %get-tuple-element.58, bf16[1024,2048]{1,0:T(8,128)(2,1)} %copy-done.9, f32[2048]{0:T(1024)S(1)} %convert_element_type.170, ...), kind=kOutput, calls=%fused_computation.36 | convolution fusion | flops 11830296576 | bytes 25702400 | tf_op jit(solution)/shard_map/dot_general | solution.py:220
  330.8 1.0 slice.93
  331.8 0.1 fusion.68
  331.9 0.1 copy.74
  332.0 0.7 copy.76
  332.7 4.0 %add_convert_fusion = bf16[16,1,256,512]{3,0,2,1:T(8,128)(2,1)S(1)} fusion(f32[16,1,256,512]{3,0,2,1:T(8,128)} %copy-done.2, f32[256,512]{1,0:T(8,128)S(1)} %bitcast.120, f32[16,256]{0,1:T(8,128)S(1)} %copy.74), kind=kLoop, calls=%fused_computation.18 | loop fusion | flops 6291456 | bytes 13123584 | tf_op jit(solution)/shard_map/convert_element_type | solution.py:225
  336.7 4.5 %copy.75 = bf16[16,1,256,512]{3,2,1,0:T(8,128)(2,1)} copy(bf16[16,1,256,512]{3,0,2,1:T(8,128)(2,1)S(1)} %add_convert_fusion) | data formatting | bytes 8388608
  341.2 5.8 %reduce-scatter.2.cloned.1.call-done = bf16[512,2048]{1,0:T(8,128)(2,1)} async-done(((bf16[1024,2048]{1,0:T(8,128)(2,1)}), bf16[512,2048]{1,0:T(8,128)(2,1)}) %reduce-scatter.2.cloned.1.call-update) | async-done | bytes 2097168 | tf_op jit(solution)/shard_map/reduce_scatter | solution.py:221
  347.0 4.4 %add_convert_fusion.1 = bf16[512,2048]{1,0:T(8,128)(2,1)} fusion(bf16[512,2048]{1,0:T(8,128)(2,1)} %reduce-scatter.2.cloned.1.call-done, bf16[1024,2048]{1,0:T(8,128)(2,1)} %copy-done.9, s32[]{:T(128)S(6)} %select_n.46), kind=kLoop, calls=%fused_computation.35 | loop fusion | flops 4194304 | bytes 6291460 | tf_op jit(solution)/shard_map/convert_element_type | solution.py:224
  (61 shorter events, 0.4 us)
Async XLA Ops:
  7.2 244.1 %copy-start = (bf16[512,2048]{1,0:T(8,128)(2,1)S(1)}, bf16[512,2048]{1,0:T(8,128)(2,1)}, u32[]{:S(2)}) copy-start(bf16[512,2048]{1,0:T(8,128)(2,1)} %param.27) | copy-start | bytes 6291460
  7.2 89.4 %all-gather.8.cloned.1.call-start = ((), (), s32[]{:S(2)}) async-start(), calls=%async_computation.3 | async-start | bytes 1310720 | tf_op jit(solution)/shard_map/all_gather | solution.py:24
  7.2 4.3 %copy-start.7 = (bf16[1024,2048]{1,0:T(8,128)(2,1)S(1)}, bf16[1024,2048]{1,0:T(8,128)(2,1)}, u32[]{:S(2)}) copy-start(bf16[1024,2048]{1,0:T(8,128)(2,1)} %param.18) | copy-start | bytes 12582916
  11.5 13.0 %copy-start.16 = (s32[1,16]{1,0:T(1,128)S(1)}, s32[1,16]{1,0:T(1,128)}, u32[]{:S(2)}) copy-start(s32[1,16]{1,0:T(1,128)} %param.33) | copy-start | bytes 196
  11.5 13.0 %copy-start.18 = (s32[1,16]{1,0:T(1,128)S(1)}, s32[1,16]{1,0:T(1,128)}, u32[]{:S(2)}) copy-start(s32[1,16]{1,0:T(1,128)} %param.32) | copy-start | bytes 196
  11.5 13.2 %copy-start.14 = (bf16[4,1024]{1,0:T(4,128)(2,1)S(1)}, bf16[4,1024]{1,0:T(4,128)(2,1)}, u32[]{:S(2)}) copy-start(bf16[4,1024]{1,0:T(4,128)(2,1)} %param.21) | copy-start | bytes 24580
  11.5 13.2 %copy-start.19 = (bf16[2048,16]{0,1:T(8,128)(2,1)S(1)}, bf16[2048,16]{0,1:T(8,128)(2,1)}, u32[]{:S(2)}) copy-start(bf16[2048,16]{0,1:T(8,128)(2,1)} %param.22) | copy-start | bytes 196612
  11.5 13.2 %copy-start.20 = (bf16[16,256]{1,0:T(8,128)(2,1)S(1)}, bf16[16,256]{1,0:T(8,128)(2,1)}, u32[]{:S(2)}) copy-start(bf16[16,256]{1,0:T(8,128)(2,1)} %param.23) | copy-start | bytes 24580
  11.6 13.2 %copy-start.21 = (f32[256]{0:T(256)S(1)}, f32[256]{0:T(256)}, u32[]{:S(2)}) copy-start(f32[256]{0:T(256)} %param.24) | copy-start | bytes 3076
  18.8 1.3 copy-start.11
  20.2 17.3 %collective-permute-start = (bf16[3,1024]{1,0:T(4,128)(2,1)S(1)}, bf16[3,1024]{1,0:T(4,128)(2,1)S(1)}, u32[]{:S(2)}, u32[]{:S(2)}) collective-permute-start(bf16[3,1024]{1,0:T(4,128)(2,1)S(1)} %slice_bitcast_fusion.5), channel_id=1, source_target_pairs={{0,2},{2,4},{4,6},{1,3},{3,5},{5,7},{8,10},{10,12},{12,14},{9,11},... | collective-permute-start | bytes 18440 | tf_op jit(solution)/shard_map/ppermute | solution.py:18
  31.8 13.5 %copy-start.5 = (f32[16,1,64,256]{3,0,1,2:T(8,128)}, f32[16,1,64,256]{3,0,1,2:T(8,128)S(1)}, u32[]{:S(2)}) copy-start(f32[16,1,64,256]{3,0,1,2:T(8,128)S(1)} %fusion.49) | copy-start | bytes 3145732
  45.3 7.4 %copy-start.3 = (f32[16,64,1,1024]{3,1,0,2:T(8,128)}, f32[16,64,1,1024]{3,1,0,2:T(8,128)S(1)}, u32[]{:S(2)}) copy-start(f32[16,64,1,1024]{3,1,0,2:T(8,128)S(1)} %fusion.15) | copy-start | bytes 12582916
  52.7 18.3 %copy-start.12 = (bf16[128,1408]{1,0:T(8,128)(2,1)S(1)}, bf16[128,1408]{1,0:T(8,128)(2,1)}, u32[]{:S(2)}) copy-start(bf16[128,1408]{1,0:T(8,128)(2,1)} %param.30) | copy-start | bytes 1081348
  52.7 18.3 %copy-start.13 = (bf16[128,1408]{1,0:T(8,128)(2,1)S(1)}, bf16[128,1408]{1,0:T(8,128)(2,1)}, u32[]{:S(2)}) copy-start(bf16[128,1408]{1,0:T(8,128)(2,1)} %param.29) | copy-start | bytes 1081348
  66.3 3.3 copy-start.2
  69.6 3.9 %copy-start.17 = (bf16[512]{0:T(512)(128)(2,1)S(1)}, bf16[512]{0:T(512)(128)(2,1)}, u32[]{:S(2)}) copy-start(bf16[512]{0:T(512)(128)(2,1)} %param.26) | copy-start | bytes 3076
  70.9 114.2 %all-gather.6.cloned.1.call-start = ((), (), s32[]{:S(2)}) async-start(), calls=%async_computation.2 | async-start | bytes 12255232 | tf_op jit(solution)/shard_map/all_gather | solution.py:154
  71.9 179.3 %all-gather.4.cloned.1.call-start = ((), (), s32[]{:S(2)}) async-start(), calls=%async_computation.1 | async-start | bytes 6127616 | tf_op jit(solution)/shard_map/all_gather | solution.py:159
  72.7 219.1 %all-reduce.3.cloned.1.call-start = ((), (), s32[]{:S(2)}) async-start(), calls=%async_computation.4 | async-start | bytes 8388608 | tf_op jit(solution)/shard_map/psum | solution.py:209
  194.5 4.8 %copy-start.4 = (f32[16,64,1,1024]{3,1,0,2:T(8,128)S(1)}, f32[16,64,1,1024]{3,1,0,2:T(8,128)}, u32[]{:S(2)}) copy-start(f32[16,64,1,1024]{3,1,0,2:T(8,128)} %copy-done.3) | copy-start | bytes 12582916
  194.5 6.7 %copy-start.6 = (f32[16,1,64,256]{3,0,1,2:T(8,128)S(1)}, f32[16,1,64,256]{3,0,1,2:T(8,128)}, u32[]{:S(2)}) copy-start(f32[16,1,64,256]{3,0,1,2:T(8,128)} %copy-done.5) | copy-start | bytes 3145732
  194.5 6.7 %copy-start.8 = (f32[16,1,64,256]{3,2,0,1:T(8,128)S(1)}, f32[16,1,64,256]{3,2,0,1:T(8,128)}, u32[]{:S(2)}) copy-start(f32[16,1,64,256]{3,2,0,1:T(8,128)} %multiply_bitcast_fusion.1) | copy-start | bytes 3145732
  217.5 1.3 copy-start.10
  256.8 0.7 copy-start.15
  256.8 90.2 %reduce-scatter.2.cloned.1.call-start = ((), (), s32[]{:S(2)}) async-start(), calls=%async_computation.5 | async-start | bytes 6291456 | tf_op jit(solution)/shard_map/reduce_scatter | solution.py:221
  297.2 1.9 copy-start.9
  336.7 14.8 %copy-start.1 = (bf16[512,2048]{1,0:T(8,128)(2,1)S(1)}, bf16[512,2048]{1,0:T(8,128)(2,1)}, u32[]{:S(2)}) copy-start(bf16[512,2048]{1,0:T(8,128)(2,1)} %param.27) | copy-start | bytes 6291460
Sparse Core Ops, SparseCore 0:
  71.0 25.4 all-gather.7
  98.7 86.3 all-gather.5
  187.3 63.9 all-gather.3
  257.0 34.7 all-reduce.2
  330.9 16.0 reduce-scatter.1
